TPU v7x, 256 devices: a whole 4x4x8 slice. The times are simulated.
256 devices in a mesh: gx: 4 (over x_lo, core), gy: 8 (over z), gz: 8 (over x_hi, y).
Axes of the slice: x: 4 (x_hi: 2, x_lo: 2; x = x_hi * 2 + x_lo), y: 4, z: 8, core: 2. Of those that a mesh axis runs over, the one named last changes fastest.
Arguments:
- traces: bfloat16 [2, 4, 8, 8, 512, 768], P(None, 'gx', 'gy', 'gz'), may hold values from -6 to 6
- sources: bfloat16 [2, 4, 8, 8, 512, 768], P(None, 'gx', 'gy', 'gz'), may hold values from -4 to 4
- local_ops: bfloat16 [2, 4, 8, 8, 768, 768], P(None, 'gx', 'gy', 'gz'), may hold values from -0.15625 to 0.15625
- plane_coupling: bfloat16 [4, 64, 64], P('gx'), may hold values from -0.375 to 0.375
- face_owner: int32 [4, 64], P('gx'), may hold values from 0 to 63, each once within a row
Outputs:
- new_traces: bfloat16 [2, 4, 8, 8, 512, 768], P(None, 'gx', 'gy', 'gz')
Inputs may be any that keep to these rules, and one draw needn't show every extreme that they name: `face_owner`: each row is a permutation of the 64 plane positions.
All inputs are finite; a program needn't handle non-finite values.
Results may differ from a plain program's by a relative error of at most 0.0062.
Values may be sent and summed in bfloat16 or wider, within the bound.
A program may use at most 64 MiB of HBM per device.

v0:
```python
import jax
import jax.numpy as jnp
from jax import lax
from jax.sharding import PartitionSpec as P

SWEEPS = 2


def with_halo(block, sides, width):
    for axis, dim in sides:
        count = lax.axis_size(axis)
        forward = [(i, i + 1) for i in range(count - 1)]
        forward.append((count - 1, 0))
        backward = [(target, source) for source, target in forward]
        low = lax.ppermute(
            lax.slice_in_dim(block, block.shape[dim] - width, None, axis=dim), axis, forward
        )
        high = lax.ppermute(lax.slice_in_dim(block, 0, width, axis=dim), axis, backward)
        block = jnp.concatenate([low, block, high], axis=dim)
    return block


def on_device(traces, sources, local_ops, plane_coupling, face_owner):
    columns_all = local_ops.shape[-1]
    slab_width = columns_all // 6
    slab_rows = traces.shape[4]
    count_y = lax.axis_size("gy")
    count_z = lax.axis_size("gz")
    plane_size = count_y * count_z
    block_rows_count = slab_rows // plane_size
    operators = local_ops.reshape(2, columns_all, columns_all)
    source_rows = sources.reshape(2, slab_rows, columns_all).astype(jnp.float32)
    incoming = traces.reshape(2, slab_rows, columns_all)
    owners = face_owner.reshape(plane_size)
    select = (owners[:, None] == jnp.arange(plane_size, dtype=jnp.int32)[None, :]).astype(
        jnp.float32
    )
    mixing = jnp.dot(
        plane_coupling.reshape(plane_size, plane_size).astype(jnp.float32),
        select,
        precision=lax.Precision.HIGHEST,
    ).astype(jnp.bfloat16)
    for sweep_step in range(SWEEPS):
        real_part = (
            jnp.dot(incoming[0], operators[0], preferred_element_type=jnp.float32)
            - jnp.dot(incoming[1], operators[1], preferred_element_type=jnp.float32)
            + source_rows[0]
        )
        imag_part = (
            jnp.dot(incoming[0], operators[1], preferred_element_type=jnp.float32)
            + jnp.dot(incoming[1], operators[0], preferred_element_type=jnp.float32)
            + source_rows[1]
        )
        outgoing = (
            jnp.stack([real_part, imag_part])
            .astype(jnp.bfloat16)
            .reshape(2, slab_rows, 6, slab_width)
        )
        along_x = with_halo(outgoing[:, :, 0:2, :], (("gx", 2),), 1)
        partial_faces = jnp.concatenate(
            [along_x[:, :, 0:1], along_x[:, :, 3:4], outgoing[:, :, 2:6]], axis=2
        )
        blocks = partial_faces.reshape(2, plane_size, block_rows_count, 6, slab_width)
        update_block_rows = lax.all_to_all(
            blocks, ("gy", "gz"), split_axis=1, concat_axis=1, tiled=True
        )
        row_count = update_block_rows.shape[2]
        grid_view = update_block_rows.reshape(2, count_y, count_z, row_count, 6, slab_width)
        moved = jnp.stack(
            [
                grid_view[:, :, :, :, 0],
                grid_view[:, :, :, :, 1],
                jnp.roll(grid_view[:, :, :, :, 3], 1, axis=1),
                jnp.roll(grid_view[:, :, :, :, 2], -1, axis=1),
                jnp.roll(grid_view[:, :, :, :, 5], 1, axis=2),
                jnp.roll(grid_view[:, :, :, :, 4], -1, axis=2),
            ],
            axis=4,
        )
        block_rows = moved.reshape(2, plane_size, row_count * columns_all)
        coupled = jnp.einsum("pq,rqc->rpc", mixing, block_rows, preferred_element_type=jnp.float32)
        updated = (block_rows.astype(jnp.float32) - coupled).astype(jnp.bfloat16)
        updated = updated.reshape(2, plane_size, row_count, 6, slab_width)
        returned = lax.all_to_all(updated, ("gy", "gz"), split_axis=1, concat_axis=1, tiled=True)
        incoming = returned.reshape(2, slab_rows, columns_all)
    return incoming.reshape(traces.shape)


def solution(mesh):
    placed = (
        P(None, "gx", "gy", "gz", None, None),
        P(None, "gx", "gy", "gz", None, None),
        P(None, "gx", "gy", "gz", None, None),
        P("gx", None, None),
        P("gx", None),
    )
    return jax.shard_map(
        on_device,
        mesh=mesh,
        in_specs=placed,
        out_specs=P(None, "gx", "gy", "gz", None, None),
        check_vma=False,
    )
```

profile of v0, /device:TPU:8, one launch (start us, length us, event | category | flops | bytes accessed | tf_op | source)
XLA Modules:
  0.0 268.1 jit_solution(3088411182501243371)
XLA Ops:
  0.0 0.0 copy-start
  0.0 2.4 fusion.15
  2.4 0.0 copy-done.1
  2.5 0.0 copy-start.8
  2.5 2.0 fusion.22
  4.5 0.0 copy-done.8
  4.5 0.0 copy-start.9
  4.5 0.2 convert_element_type.26
  4.8 1.2 copy-done.9
  5.9 1.7 add_convert_fusion.2
  7.6 1.7 add_convert_fusion.3
  9.4 2.3 copy.56
  11.7 2.3 copy.57
  14.0 1.3 pad_maximum_fusion.3
  15.3 0.1 collective-permute-start
  15.3 1.7 collective-permute-start.1
  17.1 5.1 %collective-permute-done = bf16[2,512,1,128]{1,3,2,0:T(8,128)(2,1)S(1)} collective-permute-done((bf16[2,512,1,128]{1,3,2,0:T(8,128)(2,1)S(1)}, bf16[2,512,1,128]{1,3,2,0:T(8,128)(2,1)S(1)}, u32[]{:S(2)}, u32[]{:S(2)}) %collective-permute-start) | collective-permute-done | bytes 262176 | tf_op jit(solution)/shard_map/ppermute | solution.py:15
  22.2 0.8 collective-permute-done.1
  23.0 0.0 copy-done.5
  23.0 1.3 fusion.9
  24.3 2.6 copy.58
  26.9 2.8 %copy.59 = bf16[2,64,8,6,128]{4,2,3,0,1:T(8,128)(2,1)} copy(bf16[2,64,8,6,128]{4,2,1,3,0:T(8,128)(2,1)} %bitcast.168) | data formatting | bytes 3145728 | tf_op jit(solution)/shard_map/reshape | solution.py:63
  29.7 14.6 %all-to-all-start = ((bf16[2,64,8,6,128]{4,2,3,0,1:T(8,128)(2,1)}), bf16[2,64,8,6,128]{4,2,3,0,1:T(8,128)(2,1)}, u32[]{:S(2)}, u32[]{:S(2)}) async-start(bf16[2,64,8,6,128]{4,2,3,0,1:T(8,128)(2,1)} %copy.59), calls=%async_computation | async-start | bytes 3145728 | tf_op jit(solution)/shard_map/all_to_all | solution.py:64
  44.3 0.2 fusion.24
  44.5 40.1 %all-to-all-done = bf16[2,64,8,6,128]{4,2,3,0,1:T(8,128)(2,1)} async-done(((bf16[2,64,8,6,128]{4,2,3,0,1:T(8,128)(2,1)}), bf16[2,64,8,6,128]{4,2,3,0,1:T(8,128)(2,1)}, u32[]{:S(2)}, u32[]{:S(2)}) %all-to-all-start) | async-done | bytes 1572896 | tf_op jit(solution)/shard_map/all_to_all | solution.py:64
  84.6 1.5 copy.60
  86.2 0.3 slice_bitcast_fusion.12
  86.7 0.1 fusion.41
  86.7 0.1 fusion.42
  86.8 0.1 fusion.43
  86.9 0.1 fusion.44
  87.0 0.4 copy.65
  87.4 1.8 fusion.3
  89.2 4.5 %reshape.67 = bf16[2,64,8,6,128]{4,3,2,1,0:T(8,128)(2,1)} reshape(bf16[2,64,6144]{2,1,0:T(8,128)(2,1)} %fusion.3) | data formatting | bytes 3145728 | tf_op jit(solution)/shard_map/reshape | solution.py:83
  93.7 1.9 copy.67
  95.6 0.0 copy-start.2
  95.6 48.0 %all_to_all.20 = bf16[2,64,8,6,128]{4,2,3,0,1:T(8,128)(2,1)S(1)} all-to-all(bf16[2,64,8,6,128]{4,2,3,0,1:T(8,128)(2,1)S(1)} %copy.67), channel_id=1, replica_groups=mesh['gx'=4,'gy'=8,'gz'=8] {'gy','gz'}, dimensions={1} | all-to-all | bytes 3145728 | tf_op jit(solution)/shard_map/all_to_all | solution.py:84
  143.6 0.8 fusion.12
  144.4 0.4 copy-done.7
  144.7 1.7 add_convert_fusion
  146.5 2.3 copy.71
  148.8 2.4 fusion.19
  151.2 2.9 %add_convert_fusion.1 = bf16[512,768]{1,0:T(8,128)(2,1)} fusion(f32[512,768]{1,0:T(8,128)S(1)} %fusion.19, f32[2,1,1,1,512,768]{5,4,3,2,1,0:T(8,128)S(1)} %convert_element_type.26, bf16[2,1,1,1,768,768]{5,4,3,2,1,0:T(8,128)(2,1)S(1)} %copy-done.3, bf16[2,64,8,6,128]{4,2,3,0,1:T(8,128)(2,1)} %copy-done.7), kind=kOutput, calls=%fused_computation.19 | convolution fusion | flops 605159424 | bytes 5898240 | tf_op jit(solution)/shard_map/dot_general | solution.py:46
  154.1 1.5 copy.70
  155.7 0.1 collective-permute-start.2
  155.7 1.7 collective-permute-start.3
  157.5 6.0 %collective-permute-done.2 = bf16[2,512,1,128]{1,3,2,0:T(8,128)(2,1)S(1)} collective-permute-done((bf16[2,512,1,128]{1,3,2,0:T(8,128)(2,1)S(1)}, bf16[2,512,1,128]{1,3,2,0:T(8,128)(2,1)S(1)}, u32[]{:S(2)}, u32[]{:S(2)}) %collective-permute-start.2) | collective-permute-done | bytes 262176 | tf_op jit(solution)/shard_map/ppermute | solution.py:15
  163.5 0.0 collective-permute-done.3
  163.5 0.1 fusion.11
  163.6 0.9 copy.72
  164.5 0.3 copy.73
  164.8 47.6 %all_to_all.21 = bf16[2,64,8,6,128]{4,2,3,0,1:T(8,128)(2,1)S(1)} all-to-all(bf16[2,64,8,6,128]{4,2,3,0,1:T(8,128)(2,1)S(1)} %copy.73), channel_id=1, replica_groups=mesh['gx'=4,'gy'=8,'gz'=8] {'gy','gz'}, dimensions={1} | all-to-all | bytes 3145728 | tf_op jit(solution)/shard_map/all_to_all | solution.py:64
  212.4 0.1 copy.74
  212.5 0.3 slice_bitcast_fusion.8
  213.1 0.1 fusion.45
  213.1 0.1 fusion.46
  213.2 0.1 fusion.47
  213.3 0.1 fusion.48
  213.4 0.4 copy.79
  213.8 1.8 fusion.2
  215.5 3.6 %reshape.71 = bf16[2,64,8,6,128]{4,3,2,1,0:T(8,128)(2,1)S(1)} reshape(bf16[2,64,6144]{2,1,0:T(8,128)(2,1)} %fusion.2) | data formatting | bytes 3145728 | tf_op jit(solution)/shard_map/reshape | solution.py:83
  219.1 0.3 copy.81
  219.4 47.4 %all_to_all.22 = bf16[2,64,8,6,128]{4,2,3,0,1:T(8,128)(2,1)S(1)} all-to-all(bf16[2,64,8,6,128]{4,2,3,0,1:T(8,128)(2,1)S(1)} %copy.81), channel_id=1, replica_groups=mesh['gx'=4,'gy'=8,'gz'=8] {'gy','gz'}, dimensions={1} | all-to-all | bytes 3145728 | tf_op jit(solution)/shard_map/all_to_all | solution.py:84
  266.8 1.2 copy.91
  (32 shorter events, 0.4 us)
Async XLA Ops:
  0.0 44.3 %copy-start = (bf16[1,64,64]{2,1,0:T(8,128)(2,1)S(1)}, bf16[1,64,64]{2,1,0:T(8,128)(2,1)}, u32[]{:S(2)}) copy-start(bf16[1,64,64]{2,1,0:T(8,128)(2,1)} %param.8) | copy-start | bytes 24580
  0.0 2.4 copy-start.1
  2.5 2.0 copy-start.8
  4.5 1.4 copy-start.9
  14.0 9.0 %copy-start.5 = (bf16[512,768]{0,1:T(8,128)(2,1)S(1)}, bf16[512,768]{0,1:T(8,128)(2,1)}, u32[]{:S(2)}) copy-start(bf16[512,768]{0,1:T(8,128)(2,1)} %copy.56) | copy-start | bytes 2359300
  14.0 9.0 %copy-start.6 = (bf16[512,768]{0,1:T(8,128)(2,1)S(1)}, bf16[512,768]{0,1:T(8,128)(2,1)}, u32[]{:S(2)}) copy-start(bf16[512,768]{0,1:T(8,128)(2,1)} %copy.57) | copy-start | bytes 2359300
  15.3 6.9 %collective-permute-start = (bf16[2,512,1,128]{1,3,2,0:T(8,128)(2,1)S(1)}, bf16[2,512,1,128]{1,3,2,0:T(8,128)(2,1)S(1)}, u32[]{:S(2)}, u32[]{:S(2)}) collective-permute-start(bf16[2,512,1,128]{1,3,2,0:T(8,128)(2,1)S(1)} %get-tuple-element.15), channel_id=1, source_target_pairs={{0,64},{64,128},{128,192},{192,0},{1,65},{65,129},{129,193},{193,1... | collective-permute-start | bytes 786440 | tf_op jit(solution)/shard_map/ppermute | solution.py:15
  15.3 7.6 %collective-permute-start.1 = (bf16[2,512,1,128]{1,3,2,0:T(8,128)(2,1)S(1)}, bf16[2,512,1,128]{1,3,2,0:T(8,128)(2,1)S(1)}, u32[]{:S(2)}, u32[]{:S(2)}) collective-permute-start(bf16[2,512,1,128]{1,3,2,0:T(8,128)(2,1)S(1)} %get-tuple-element.16), channel_id=1, source_target_pairs={{64,0},{128,64},{192,128},{0,192},{65,1},{129,65},{193,129},{1,193... | collective-permute-start | bytes 786440 | tf_op jit(solution)/shard_map/ppermute | solution.py:18
  29.7 14.6 %copy-start.10 = (s32[1,64]{1,0:T(1,128)S(1)}, s32[1,64]{1,0:T(1,128)}, u32[]{:S(2)}) copy-start(s32[1,64]{1,0:T(1,128)} %param.9) | copy-start | bytes 772
  29.7 54.9 %all-to-all-start = ((bf16[2,64,8,6,128]{4,2,3,0,1:T(8,128)(2,1)}), bf16[2,64,8,6,128]{4,2,3,0,1:T(8,128)(2,1)}, u32[]{:S(2)}, u32[]{:S(2)}) async-start(bf16[2,64,8,6,128]{4,2,3,0,1:T(8,128)(2,1)} %copy.59), calls=%async_computation | async-start | bytes 3145728 | tf_op jit(solution)/shard_map/all_to_all | solution.py:64
  95.6 48.0 %copy-start.2 = (bf16[2,1,1,1,768,768]{5,4,3,2,1,0:T(8,128)(2,1)S(1)}, bf16[2,1,1,1,768,768]{5,4,3,2,1,0:T(8,128)(2,1)}, u32[]{:S(2)}) copy-start(bf16[2,1,1,1,768,768]{5,4,3,2,1,0:T(8,128)(2,1)} %param.7) | copy-start | bytes 7077892
  143.6 1.1 copy-start.7
  148.8 2.5 copy-start.3
  154.1 1.5 copy-start.4
  155.7 7.8 %collective-permute-start.2 = (bf16[2,512,1,128]{1,3,2,0:T(8,128)(2,1)S(1)}, bf16[2,512,1,128]{1,3,2,0:T(8,128)(2,1)S(1)}, u32[]{:S(2)}, u32[]{:S(2)}) collective-permute-start(bf16[2,512,1,128]{1,3,2,0:T(8,128)(2,1)S(1)} %get-tuple-element.9), channel_id=1, source_target_pairs={{0,64},{64,128},{128,192},{192,0},{1,65},{65,129},{129,193},{193,1... | collective-permute-start | bytes 786440 | tf_op jit(solution)/shard_map/ppermute | solution.py:15
  155.7 7.7 %collective-permute-start.3 = (bf16[2,512,1,128]{1,3,2,0:T(8,128)(2,1)S(1)}, bf16[2,512,1,128]{1,3,2,0:T(8,128)(2,1)S(1)}, u32[]{:S(2)}, u32[]{:S(2)}) collective-permute-start(bf16[2,512,1,128]{1,3,2,0:T(8,128)(2,1)S(1)} %get-tuple-element.10), channel_id=1, source_target_pairs={{64,0},{128,64},{192,128},{0,192},{65,1},{129,65},{193,129},{1,193... | collective-permute-start | bytes 786440 | tf_op jit(solution)/shard_map/ppermute | solution.py:18
where the time goes:
time: 269 us; the launch traced here: 268 us
  blocking collectives  143 us (53%)
  waiting for transfers between devices  52 us (19%)
  local copies, waits for them, and re-layouts  31.3 us (12%)
  matrix products  19.5 us (7%)
  starting transfers between devices  18.2 us (7%)
  other arithmetic  3.57 us (1%)
    all_to_all x2, blocking collectives, on_device(): lax.all_to_all(updated, ('gy', 'gz'), split_axis=1, concat_axis=1, tiled=...  95.4 us
    all_to_all x1, blocking collectives, on_device(): lax.all_to_all(blocks, ('gy', 'gz'), split_axis=1, concat_axis=1, tiled=T...  47.6 us
    all_to_all x1, waiting for transfers between devices, on_device(): lax.all_to_all(blocks, ('gy', 'gz'), split_axis=1, concat_axis=1, tiled=T...  40.1 us
    all_to_all x1, starting transfers between devices, on_device(): lax.all_to_all(blocks, ('gy', 'gz'), split_axis=1, concat_axis=1, tiled=T...  14.6 us
    ppermute x2, waiting for transfers between devices, with_halo(): lax.ppermute(lax.slice_in_dim(block, block.shape[dim] - width, None, axis...  11.1 us
    reshape x4, local copies, waits for them, and re-layouts, on_device(): updated = updated.reshape(2, plane_size, row_count, 6, slab_width)  10.2 us
    another operation x4, local copies, waits for them, and re-layouts  8.4 us
  transfers between devices with their start and end apart: 5, of which 4 were waited for; matrix products, arithmetic and copies ran while one was open for 0% of the time, Pallas kernels for 0%

commit v1 on v0

--- a/solution.py
+++ b/solution.py
@@ -1,9 +1,26 @@
+import functools
 import jax
 import jax.numpy as jnp
 from jax import lax
 from jax.sharding import PartitionSpec as P
+from jax.lax import all_to_all, psum
 
 SWEEPS = 2
+
+
+def lay_the_pools(xs, lane_axis, d_out, array_dim):
+    return jnp.concatenate(
+        all_to_all(
+            jnp.stack(jnp.split(xs, psum(1, lane_axis), axis=d_out), axis=0),
+            lane_axis,
+            split_axis=0,
+            concat_axis=0,
+        ),
+        axis=array_dim,
+    )
+
+
+_obtain_region = functools.partial(lay_the_pools, lane_axis=("gy", "gz"), d_out=1, array_dim=1)
 
 
 def with_halo(block, sides, width):
@@ -81,7 +98,7 @@
         coupled = jnp.einsum("pq,rqc->rpc", mixing, block_rows, preferred_element_type=jnp.float32)
         updated = (block_rows.astype(jnp.float32) - coupled).astype(jnp.bfloat16)
         updated = updated.reshape(2, plane_size, row_count, 6, slab_width)
-        returned = lax.all_to_all(updated, ("gy", "gz"), split_axis=1, concat_axis=1, tiled=True)
+        returned = _obtain_region(updated)
         incoming = returned.reshape(2, slab_rows, columns_all)
     return incoming.reshape(traces.shape)
 

time: 269 us -> 325 us (1.21); the launches traced: 268 us -> 319 us
  local copies, waits for them, and re-layouts: 31.3 us -> 82.2 us
    unnamed x24 -> x150, local copies, waits for them, and re-layouts: 1.65 us -> 53.1 us
    reshape x4 -> x2, local copies, waits for them, and re-layouts: 10.2 us -> 8.09 us  [on_device(): updated = updated.reshape(2, plane_size, row_count, 6, slab_width)]
    another operation x4 -> x8, local copies, waits for them, and re-layouts: 8.4 us -> 9.87 us
where the time goes in v1:
time: 325 us; the launch traced here: 319 us
  blocking collectives  143 us (44%)
  local copies, waits for them, and re-layouts  82.2 us (25%)
  waiting for transfers between devices  52 us (16%)
  matrix products  19.8 us (6%)
  starting transfers between devices  18.2 us (6%)
  other arithmetic  3.57 us (1%)
    all_to_all x2, blocking collectives, lay_the_pools(): all_to_all(jnp.stack(jnp.split(xs, psum(1, lane_axis), axis=d_out), axis=...  95.3 us
    unnamed x150, local copies, waits for them, and re-layouts  53.1 us
    all_to_all x1, blocking collectives, on_device(): lax.all_to_all(blocks, ('gy', 'gz'), split_axis=1, concat_axis=1, tiled=T...  47.6 us
    all_to_all x1, waiting for transfers between devices, on_device(): lax.all_to_all(blocks, ('gy', 'gz'), split_axis=1, concat_axis=1, tiled=T...  40.1 us
    all_to_all x1, starting transfers between devices, on_device(): lax.all_to_all(blocks, ('gy', 'gz'), split_axis=1, concat_axis=1, tiled=T...  14.6 us
    ppermute x2, waiting for transfers between devices, with_halo(): lax.ppermute(lax.slice_in_dim(block, block.shape[dim] - width, None, axis...  11.1 us
    another operation x4, local copies, waits for them, and re-layouts  8.39 us
    reshape x2, local copies, waits for them, and re-layouts, on_device(): updated = updated.reshape(2, plane_size, row_count, 6, slab_width)  8.09 us
  transfers between devices with their start and end apart: 5, of which 4 were waited for; matrix products, arithmetic and copies ran while one was open for 0% of the time, Pallas kernels for 0%

profile of v1, /device:TPU:8, one launch (start us, length us, event | category | flops | bytes accessed | tf_op | source)
XLA Modules:
  0.0 319.4 jit_solution(12081410061274300644)
XLA Ops:
  0.0 2.4 fusion.15
  2.5 2.0 fusion.22
  4.8 1.2 copy-done.9
  5.9 1.7 add_convert_fusion.2
  7.6 1.7 add_convert_fusion.3
  9.4 2.3 copy.435
  11.7 2.3 copy.436
  14.0 1.3 pad_maximum_fusion.3
  15.3 1.7 collective-permute-start.1
  17.1 5.1 %collective-permute-done = bf16[2,512,1,128]{1,3,2,0:T(8,128)(2,1)S(1)} collective-permute-done((bf16[2,512,1,128]{1,3,2,0:T(8,128)(2,1)S(1)}, bf16[2,512,1,128]{1,3,2,0:T(8,128)(2,1)S(1)}, u32[]{:S(2)}, u32[]{:S(2)}) %collective-permute-start) | collective-permute-done | bytes 262176 | tf_op jit(solution)/shard_map/ppermute | solution.py:32
  22.2 0.8 collective-permute-done.1
  23.0 1.3 fusion.9
  24.3 2.6 copy.437
  26.9 2.8 copy.438
  29.7 14.6 %all-to-all-start = ((bf16[2,64,8,6,128]{4,2,3,0,1:T(8,128)(2,1)}), bf16[2,64,8,6,128]{4,2,3,0,1:T(8,128)(2,1)}, u32[]{:S(2)}, u32[]{:S(2)}) async-start(bf16[2,64,8,6,128]{4,2,3,0,1:T(8,128)(2,1)} %copy.438), calls=%async_computation | async-start | bytes 3145728 | tf_op jit(solution)/shard_map/all_to_all | solution.py:81
  44.5 40.1 %all-to-all-done = bf16[2,64,8,6,128]{4,2,3,0,1:T(8,128)(2,1)} async-done(((bf16[2,64,8,6,128]{4,2,3,0,1:T(8,128)(2,1)}), bf16[2,64,8,6,128]{4,2,3,0,1:T(8,128)(2,1)}, u32[]{:S(2)}, u32[]{:S(2)}) %all-to-all-start) | async-done | bytes 1572896 | tf_op jit(solution)/shard_map/all_to_all | solution.py:81
  84.6 1.5 copy.439
  87.4 1.8 fusion.3
  89.2 4.5 %reshape.72 = bf16[2,64,8,6,128]{4,3,2,1,0:T(8,128)(2,1)} reshape(bf16[2,64,6144]{2,1,0:T(8,128)(2,1)} %fusion.3) | data formatting | bytes 3145728 | tf_op jit(solution)/shard_map/reshape | solution.py:100
  95.2 0.8 constant_dynamic-update-slice_fusion.65
  96.0 0.8 constant_dynamic-update-slice_fusion.64
  96.8 0.8 constant_dynamic-update-slice_fusion.63
  97.6 0.8 constant_dynamic-update-slice_fusion.62
  98.3 0.8 constant_dynamic-update-slice_fusion.61
  99.9 0.8 constant_dynamic-update-slice_fusion.59
  103.0 0.8 constant_dynamic-update-slice_fusion.55
  105.3 0.8 constant_dynamic-update-slice_fusion.52
  106.1 0.8 constant_dynamic-update-slice_fusion.51
  108.5 0.8 constant_dynamic-update-slice_fusion.48
  109.2 0.8 constant_dynamic-update-slice_fusion.47
  111.6 0.8 constant_dynamic-update-slice_fusion.44
  112.3 0.8 constant_dynamic-update-slice_fusion.43
  114.7 0.8 constant_dynamic-update-slice_fusion.40
  117.8 0.8 constant_dynamic-update-slice_fusion.36
  120.1 0.8 constant_dynamic-update-slice_fusion.33
  120.9 0.8 constant_dynamic-update-slice_fusion.32
  123.2 0.8 constant_dynamic-update-slice_fusion.29
  124.0 0.8 constant_dynamic-update-slice_fusion.28
  126.3 0.8 constant_dynamic-update-slice_fusion.25
  127.1 0.8 constant_dynamic-update-slice_fusion.24
  129.5 0.8 constant_dynamic-update-slice_fusion.21
  132.6 0.8 constant_dynamic-update-slice_fusion.17
  134.9 0.8 constant_dynamic-update-slice_fusion.14
  135.7 0.8 constant_dynamic-update-slice_fusion.13
  138.0 0.8 constant_dynamic-update-slice_fusion.10
  138.8 0.8 constant_dynamic-update-slice_fusion.9
  141.1 0.8 constant_dynamic-update-slice_fusion.6
  141.9 0.8 constant_dynamic-update-slice_fusion.5
  143.8 47.9 %all_to_all.20 = bf16[64,2,1,8,6,128]{5,3,4,2,1,0:T(8,128)(2,1)S(1)} all-to-all(bf16[64,2,1,8,6,128]{5,3,4,2,1,0:T(8,128)(2,1)S(1)} %copy.509), channel_id=1, replica_groups=mesh['gx'=4,'gy'=8,'gz'=8] {'gy','gz'}, dimensions={0} | all-to-all | bytes 3145728 | tf_op jit(solution)/shard_map/all_to_all | solution.py:13
  191.8 2.1 copy-done.3
  193.9 0.8 fusion.12
  194.7 1.9 fusion.19
  196.6 1.7 add_convert_fusion
  198.4 2.3 copy.512
  200.6 3.7 %add_convert_fusion.1 = bf16[512,768]{1,0:T(8,128)(2,1)} fusion(f32[512,768]{1,0:T(8,128)} %fusion.19, f32[2,1,1,1,512,768]{5,4,3,2,1,0:T(8,128)S(1)} %convert_element_type.26, bf16[2,1,1,1,768,768]{5,4,3,2,1,0:T(8,128)(2,1)} %param.7, bf16[2,64,1,8,6,128]{5,3,4,2,1,0:T(8,128)(2,1)} %bitcast.938), kind=kOutput, calls=%fused_computation.20 | convolution fusion | flops 605159424 | bytes 5898240 | tf_op jit(solution)/shard_map/dot_general | solution.py:63
  204.3 1.5 copy.511
  206.0 1.7 collective-permute-start.3
  207.7 6.0 %collective-permute-done.2 = bf16[2,512,1,128]{1,3,2,0:T(8,128)(2,1)S(1)} collective-permute-done((bf16[2,512,1,128]{1,3,2,0:T(8,128)(2,1)S(1)}, bf16[2,512,1,128]{1,3,2,0:T(8,128)(2,1)S(1)}, u32[]{:S(2)}, u32[]{:S(2)}) %collective-permute-start.2) | collective-permute-done | bytes 262176 | tf_op jit(solution)/shard_map/ppermute | solution.py:32
  213.8 0.9 copy.513
  215.0 47.6 %all_to_all.21 = bf16[2,64,8,6,128]{4,2,3,0,1:T(8,128)(2,1)S(1)} all-to-all(bf16[2,64,8,6,128]{4,2,3,0,1:T(8,128)(2,1)S(1)} %copy.514), channel_id=1, replica_groups=mesh['gx'=4,'gy'=8,'gz'=8] {'gy','gz'}, dimensions={1} | all-to-all | bytes 3145728 | tf_op jit(solution)/shard_map/all_to_all | solution.py:81
  264.0 1.8 fusion.2
  265.8 3.6 %reshape.77 = bf16[2,64,8,6,128]{4,3,2,1,0:T(8,128)(2,1)S(1)} reshape(bf16[2,64,6144]{2,1,0:T(8,128)(2,1)} %fusion.2) | data formatting | bytes 3145728 | tf_op jit(solution)/shard_map/reshape | solution.py:100
  270.7 47.4 %all_to_all.22 = bf16[64,2,1,8,6,128]{5,3,4,2,1,0:T(8,128)(2,1)S(1)} all-to-all(bf16[64,2,1,8,6,128]{5,3,4,2,1,0:T(8,128)(2,1)S(1)} %copy.585), channel_id=1, replica_groups=mesh['gx'=4,'gy'=8,'gz'=8] {'gy','gz'}, dimensions={0} | all-to-all | bytes 3145728 | tf_op jit(solution)/shard_map/all_to_all | solution.py:13
  318.1 1.2 copy.720
  (161 shorter events, 32.2 us)
Async XLA Ops:
  0.0 44.3 %copy-start = (bf16[1,64,64]{2,1,0:T(8,128)(2,1)S(1)}, bf16[1,64,64]{2,1,0:T(8,128)(2,1)}, u32[]{:S(2)}) copy-start(bf16[1,64,64]{2,1,0:T(8,128)(2,1)} %param.8) | copy-start | bytes 24580
  0.0 2.4 copy-start.2
  2.5 2.0 copy-start.8
  4.5 1.4 copy-start.9
  14.0 9.0 %copy-start.5 = (bf16[512,768]{0,1:T(8,128)(2,1)S(1)}, bf16[512,768]{0,1:T(8,128)(2,1)}, u32[]{:S(2)}) copy-start(bf16[512,768]{0,1:T(8,128)(2,1)} %copy.435) | copy-start | bytes 2359300
  14.0 9.0 %copy-start.6 = (bf16[512,768]{0,1:T(8,128)(2,1)S(1)}, bf16[512,768]{0,1:T(8,128)(2,1)}, u32[]{:S(2)}) copy-start(bf16[512,768]{0,1:T(8,128)(2,1)} %copy.436) | copy-start | bytes 2359300
  15.3 6.9 %collective-permute-start = (bf16[2,512,1,128]{1,3,2,0:T(8,128)(2,1)S(1)}, bf16[2,512,1,128]{1,3,2,0:T(8,128)(2,1)S(1)}, u32[]{:S(2)}, u32[]{:S(2)}) collective-permute-start(bf16[2,512,1,128]{1,3,2,0:T(8,128)(2,1)S(1)} %get-tuple-element.15), channel_id=1, source_target_pairs={{0,64},{64,128},{128,192},{192,0},{1,65},{65,129},{129,193},{193,1... | collective-permute-start | bytes 786440 | tf_op jit(solution)/shard_map/ppermute | solution.py:32
  15.3 7.6 %collective-permute-start.1 = (bf16[2,512,1,128]{1,3,2,0:T(8,128)(2,1)S(1)}, bf16[2,512,1,128]{1,3,2,0:T(8,128)(2,1)S(1)}, u32[]{:S(2)}, u32[]{:S(2)}) collective-permute-start(bf16[2,512,1,128]{1,3,2,0:T(8,128)(2,1)S(1)} %get-tuple-element.16), channel_id=1, source_target_pairs={{64,0},{128,64},{192,128},{0,192},{65,1},{129,65},{193,129},{1,193... | collective-permute-start | bytes 786440 | tf_op jit(solution)/shard_map/ppermute | solution.py:35
  29.7 14.6 %copy-start.10 = (s32[1,64]{1,0:T(1,128)S(1)}, s32[1,64]{1,0:T(1,128)}, u32[]{:S(2)}) copy-start(s32[1,64]{1,0:T(1,128)} %param.9) | copy-start | bytes 772
  29.7 54.9 %all-to-all-start = ((bf16[2,64,8,6,128]{4,2,3,0,1:T(8,128)(2,1)}), bf16[2,64,8,6,128]{4,2,3,0,1:T(8,128)(2,1)}, u32[]{:S(2)}, u32[]{:S(2)}) async-start(bf16[2,64,8,6,128]{4,2,3,0,1:T(8,128)(2,1)} %copy.438), calls=%async_computation | async-start | bytes 3145728 | tf_op jit(solution)/shard_map/all_to_all | solution.py:81
  191.7 2.2 copy-start.3
  191.8 4.9 %copy-start.7 = (bf16[64,2,1,8,6,128]{5,3,4,2,0,1:T(8,128)(2,1)}, bf16[64,2,1,8,6,128]{5,3,4,2,0,1:T(8,128)(2,1)S(1)}, u32[]{:S(2)}) copy-start(bf16[64,2,1,8,6,128]{5,3,4,2,0,1:T(8,128)(2,1)S(1)} %copy.721) | copy-start | bytes 4718596
  204.3 1.5 copy-start.4
  205.9 7.8 %collective-permute-start.2 = (bf16[2,512,1,128]{1,3,2,0:T(8,128)(2,1)S(1)}, bf16[2,512,1,128]{1,3,2,0:T(8,128)(2,1)S(1)}, u32[]{:S(2)}, u32[]{:S(2)}) collective-permute-start(bf16[2,512,1,128]{1,3,2,0:T(8,128)(2,1)S(1)} %get-tuple-element.9), channel_id=1, source_target_pairs={{0,64},{64,128},{128,192},{192,0},{1,65},{65,129},{129,193},{193,1... | collective-permute-start | bytes 786440 | tf_op jit(solution)/shard_map/ppermute | solution.py:32
  206.0 7.7 %collective-permute-start.3 = (bf16[2,512,1,128]{1,3,2,0:T(8,128)(2,1)S(1)}, bf16[2,512,1,128]{1,3,2,0:T(8,128)(2,1)S(1)}, u32[]{:S(2)}, u32[]{:S(2)}) collective-permute-start(bf16[2,512,1,128]{1,3,2,0:T(8,128)(2,1)S(1)} %get-tuple-element.10), channel_id=1, source_target_pairs={{64,0},{128,64},{192,128},{0,192},{65,1},{129,65},{193,129},{1,193... | collective-permute-start | bytes 786440 | tf_op jit(solution)/shard_map/ppermute | solution.py:35
  270.7 48.7 %copy-start.1 = (bf16[1,64,64]{2,1,0:T(8,128)(2,1)S(1)}, bf16[1,64,64]{2,1,0:T(8,128)(2,1)}, u32[]{:S(2)}) copy-start(bf16[1,64,64]{2,1,0:T(8,128)(2,1)} %param.8) | copy-start | bytes 24580
